TPU v7x, 32 devices: a whole 2x2x4 slice. The times are simulated.
32 devices in a mesh: tm: 8 (over z, x), chan: 4 (over y, core).
Axes of the slice: x: 2, y: 2, z: 4, core: 2. Of those that a mesh axis runs over, the one named last changes fastest.
Arguments:
- samples: bfloat16 [4096, 16384], P('tm', 'chan'), may hold values from -180 to 180
- sketch: bfloat16 [16384, 512], P('chan'), may hold values from -0.046875 to 0.046875
Outputs:
- coords: float32 [4096, 512], P('tm')
- weights: float32 [4096], P('tm')
All inputs are finite; a program needn't handle non-finite values.
Results may differ from a plain program's by a relative error of at most 0.0033.
Values may be sent and summed in bfloat16 or wider, within the bound.
A program may use at most 64 MiB of HBM per device.

v0:
```python
import jax
import jax.numpy as jnp
from jax import lax
from jax.sharding import PartitionSpec as P

ROUNDS = 2


def shards(samples, sketch, channels):
    rows, rank = (samples.shape[0], sketch.shape[1])
    f32 = jnp.float32
    wide = samples.astype(f32)
    norms = jnp.sum(wide * wide, axis=1)
    local = jnp.dot(samples, sketch, preferred_element_type=f32)
    both = jnp.concatenate([local, jnp.broadcast_to(norms[:, None], (rows, 128))], axis=1)
    both = lax.psum(both, "chan")
    sketched, norms = (both[:, :rank], both[:, rank])
    weights = jnp.ones((rows,), f32)
    for step in range(ROUNDS):
        weighted = ((weights * weights)[:, None] * sketched).astype(jnp.bfloat16)
        local_factor = jnp.einsum("sc,sk->ck", samples, weighted, preferred_element_type=f32)
        part = lax.psum_scatter(
            local_factor.astype(jnp.bfloat16), "tm", scatter_dimension=0, tiled=True
        )
        factor = lax.all_gather(part, "tm", axis=0, tiled=True)
        gram = jnp.einsum("ck,cl->kl", factor, factor, preferred_element_type=f32)
        seen = jnp.dot(samples, factor, preferred_element_type=f32)
        both = lax.psum(jnp.concatenate([gram, seen], axis=0), "chan")
        gram, seen = (both[:rank], both[rank:])
        lower = jnp.linalg.cholesky(gram)
        coords = lax.linalg.triangular_solve(
            lower, seen, left_side=False, lower=True, transpose_a=True
        )
        energy = jnp.maximum(norms - jnp.sum(coords * coords, axis=1), 0.0)
        weights = jnp.minimum(1.0, 3.0 / jnp.sqrt(energy / channels + 1e-06))
    return (coords, weights)


def solution(mesh):
    in_specs = (P("tm", "chan"), P("chan", None))
    out_specs = (P("tm", None), P("tm"))

    def whole(samples, sketch):
        f = lambda a, b: shards(a, b, samples.shape[1])
        return jax.shard_map(f, mesh=mesh, in_specs=in_specs, out_specs=out_specs, check_vma=False)(
            samples, sketch
        )

    return whole
```

profile of v0, /device:TPU:0, one launch (start us, length us, event | category | flops | bytes accessed | tf_op | source)
XLA Modules:
  0.0 830.5 jit_solution(8468604616008280250)
XLA Ops:
  16.5 41.8 %all-reduce.5.cloned.1.call-done = f32[512,640]{0,1:T(8,128)} async-done(((f32[512,640]{0,1:T(8,128)}), f32[512,640]{0,1:T(8,128)}) %all-reduce.5.cloned.1.call-update) | async-done | bytes 1310736 | tf_op jit(solution)/shard_map/psum | solution.py:16
  65.2 88.6 %reduce-scatter.3.cloned.1.call-done = bf16[512,512]{0,1:T(8,128)(2,1)} async-done(((bf16[4096,512]{0,1:T(8,128)(2,1)}), bf16[512,512]{0,1:T(8,128)(2,1)}) %reduce-scatter.3.cloned.1.call-update) | async-done | bytes 524304 | tf_op jit(solution)/shard_map/reduce_scatter | solution.py:22
  153.9 77.0 %all-gather.3.cloned.1.call-done = bf16[4096,512]{0,1:T(8,128)(2,1)} async-done(((bf16[512,512]{0,1:T(8,128)(2,1)}), bf16[4096,512]{0,1:T(8,128)(2,1)}) %all-gather.3.cloned.1.call-update) | async-done | bytes 4194320 | tf_op jit(solution)/shard_map/all_gather | solution.py:25
  241.2 49.2 %all-reduce.7.cloned.1.call-done = f32[1024,512]{0,1:T(8,128)} async-done(((f32[1024,512]{0,1:T(8,128)}), f32[1024,512]{0,1:T(8,128)}) %all-reduce.7.cloned.1.call-update) | async-done | bytes 2097168 | tf_op jit(solution)/shard_map/psum | solution.py:28
  295.6 11.7 %cholesky.286 = f32[128,128]{1,0:T(8,128)S(1)} custom-call(f32[128,128]{1,0:T(8,128)S(1)} %cholesky.426), custom_call_target="Cholesky" | custom-call | tf_op jit(solution)/shard_map/jit(cholesky)/cholesky | solution.py:30
  307.3 9.8 %custom-call.27 = f32[1,128,128]{1,2,0:T(8,128)S(1)} custom-call(f32[1,128,128]{2,1,0:T(8,128)S(1)} %get-tuple-element.65), custom_call_target="InvertDiagBlocksLowerTriangular" | custom-call | tf_op jit(solution)/shard_map/jit(cholesky)/cholesky | solution.py:30
  319.8 11.7 %cholesky.305 = f32[128,128]{1,0:T(8,128)S(1)} custom-call(f32[128,128]{1,0:T(8,128)S(1)} %cholesky.430), custom_call_target="Cholesky" | custom-call | tf_op jit(solution)/shard_map/jit(cholesky)/cholesky | solution.py:30
  331.6 10.0 %custom-call.28 = f32[1,128,128]{1,2,0:T(8,128)S(1)} custom-call(f32[1,128,128]{2,1,0:T(8,128)S(1)} %get-tuple-element.62), custom_call_target="InvertDiagBlocksLowerTriangular" | custom-call | tf_op jit(solution)/shard_map/jit(cholesky)/cholesky | solution.py:30
  343.1 11.7 %cholesky.326 = f32[128,128]{1,0:T(8,128)S(1)} custom-call(f32[128,128]{1,0:T(8,128)S(1)} %cholesky.435), custom_call_target="Cholesky" | custom-call | tf_op jit(solution)/shard_map/jit(cholesky)/cholesky | solution.py:30
  355.5 9.8 %custom-call.29 = f32[1,128,128]{1,2,0:T(8,128)S(1)} custom-call(f32[1,128,128]{2,1,0:T(8,128)S(1)} %get-tuple-element.59), custom_call_target="InvertDiagBlocksLowerTriangular" | custom-call | tf_op jit(solution)/shard_map/jit(cholesky)/cholesky | solution.py:30
  366.8 11.7 %cholesky.343 = f32[128,128]{1,0:T(8,128)S(1)} custom-call(f32[128,128]{1,0:T(8,128)S(1)} %convolution_subtract_fusion.11), custom_call_target="Cholesky" | custom-call | tf_op jit(solution)/shard_map/jit(cholesky)/cholesky | solution.py:30
  383.7 11.7 %while.4 = (s32[]{:T(128)}, f32[512,512]{1,0:T(8,128)}, s32[4,2]{0,1:T(2,128)S(1)}, f32[4,128,128]{2,1,0:T(8,128)S(1)}, s32[]{:T(128)}) while((s32[]{:T(128)}, f32[512,512]{1,0:T(8,128)}, s32[4,2]{0,1:T(2,128)S(1)}, f32[4,128,128]{2,1,0:T(8,128)S(1)}, s32[]{:T(128)}) %tuple.58), condition=%wide.while_cond, body=%wide.while_body.sunk | while | flops 2 | bytes 131181 | solution.py:31
  395.4 39.3 %custom-call.30 = f32[4,128,128]{1,2,0:T(8,128)S(1)} custom-call(f32[4,128,128]{2,1,0:T(8,128)S(1)} %get-tuple-element.18), custom_call_target="InvertDiagBlocksLowerTriangular" | custom-call | tf_op jit(solution)/shard_map/triangular_solve/custom-call.3 | solution.py:31
  445.4 88.6 %reduce-scatter.5.cloned.1.call-done = bf16[512,512]{0,1:T(8,128)(2,1)} async-done(((bf16[4096,512]{0,1:T(8,128)(2,1)}), bf16[512,512]{0,1:T(8,128)(2,1)}) %reduce-scatter.5.cloned.1.call-update) | async-done | bytes 524304 | tf_op jit(solution)/shard_map/reduce_scatter | solution.py:22
  534.5 76.4 %all-gather.5.cloned.1.call-done = bf16[4096,512]{0,1:T(8,128)(2,1)} async-done(((bf16[512,512]{0,1:T(8,128)(2,1)}), bf16[4096,512]{0,1:T(8,128)(2,1)}) %all-gather.5.cloned.1.call-update) | async-done | bytes 4194320 | tf_op jit(solution)/shard_map/all_gather | solution.py:25
  620.7 49.7 %all-reduce.9.cloned.1.call-done = f32[1024,512]{0,1:T(8,128)} async-done(((f32[1024,512]{0,1:T(8,128)}), f32[1024,512]{0,1:T(8,128)}) %all-reduce.9.cloned.1.call-update) | async-done | bytes 2097168 | tf_op jit(solution)/shard_map/psum | solution.py:28
  675.7 11.7 %cholesky.358 = f32[128,128]{1,0:T(8,128)S(1)} custom-call(f32[128,128]{1,0:T(8,128)S(1)} %cholesky.439), custom_call_target="Cholesky" | custom-call | tf_op jit(solution)/shard_map/jit(cholesky)/cholesky | solution.py:30
  687.5 9.8 %custom-call.31 = f32[1,128,128]{1,2,0:T(8,128)S(1)} custom-call(f32[1,128,128]{2,1,0:T(8,128)S(1)} %get-tuple-element.55), custom_call_target="InvertDiagBlocksLowerTriangular" | custom-call | tf_op jit(solution)/shard_map/jit(cholesky)/cholesky | solution.py:30
  699.9 11.9 %cholesky.377 = f32[128,128]{1,0:T(8,128)S(1)} custom-call(f32[128,128]{1,0:T(8,128)S(1)} %cholesky.443), custom_call_target="Cholesky" | custom-call | tf_op jit(solution)/shard_map/jit(cholesky)/cholesky | solution.py:30
  724.5 11.7 %cholesky.398 = f32[128,128]{1,0:T(8,128)S(1)} custom-call(f32[128,128]{1,0:T(8,128)S(1)} %cholesky.448), custom_call_target="Cholesky" | custom-call | tf_op jit(solution)/shard_map/jit(cholesky)/cholesky | solution.py:30
  736.9 9.8 %custom-call.33 = f32[1,128,128]{1,2,0:T(8,128)S(1)} custom-call(f32[1,128,128]{2,1,0:T(8,128)S(1)} %get-tuple-element.49), custom_call_target="InvertDiagBlocksLowerTriangular" | custom-call | tf_op jit(solution)/shard_map/jit(cholesky)/cholesky | solution.py:30
  748.4 11.7 %cholesky.415 = f32[128,128]{1,0:T(8,128)S(1)} custom-call(f32[128,128]{1,0:T(8,128)S(1)} %convolution_subtract_fusion.10), custom_call_target="Cholesky" | custom-call | tf_op jit(solution)/shard_map/jit(cholesky)/cholesky | solution.py:30
  764.4 11.7 %while.5 = (s32[]{:T(128)}, f32[512,512]{1,0:T(8,128)}, s32[4,2]{0,1:T(2,128)S(1)}, f32[4,128,128]{2,1,0:T(8,128)S(1)}, s32[]{:T(128)}) while((s32[]{:T(128)}, f32[512,512]{1,0:T(8,128)}, s32[4,2]{0,1:T(2,128)S(1)}, f32[4,128,128]{2,1,0:T(8,128)S(1)}, s32[]{:T(128)}) %tuple.78), condition=%wide.while_cond.clone, body=%wide.while_body.clone.sunk | while | flops 2 | bytes 131181 | solution.py:31
  776.2 39.3 %custom-call.34 = f32[4,128,128]{1,2,0:T(8,128)S(1)} custom-call(f32[4,128,128]{2,1,0:T(8,128)S(1)} %get-tuple-element.19), custom_call_target="InvertDiagBlocksLowerTriangular" | custom-call | tf_op jit(solution)/shard_map/triangular_solve/custom-call.3 | solution.py:31
  (135 shorter events, 117.4 us)
Async XLA Ops:
  7.2 51.1 %all-reduce.5.cloned.1.call-start = ((), (), s32[]{:S(2)}) async-start(), calls=%async_computation.2 | async-start | bytes 2621440 | tf_op jit(solution)/shard_map/psum | solution.py:16
  7.2 3.5 copy-start.2
  16.5 137.3 %reduce-scatter.3.cloned.1.call-start = ((), (), s32[]{:S(2)}) async-start(), calls=%async_computation.3 | async-start | bytes 4718592 | tf_op jit(solution)/shard_map/reduce_scatter | solution.py:22
  65.1 165.7 %all-gather.3.cloned.1.call-start = ((), (), s32[]{:S(2)}) async-start(), calls=%async_computation.4 | async-start | bytes 4718592 | tf_op jit(solution)/shard_map/all_gather | solution.py:25
  153.8 136.6 %all-reduce.7.cloned.1.call-start = ((), (), s32[]{:S(2)}) async-start(), calls=%async_computation.5 | async-start | bytes 4194304 | tf_op jit(solution)/shard_map/psum | solution.py:28
  230.8 6.0 copy-start.7
  240.7 293.3 %reduce-scatter.5.cloned.1.call-start = ((), (), s32[]{:S(2)}) async-start(), calls=%async_computation.6 | async-start | bytes 4718592 | tf_op jit(solution)/shard_map/reduce_scatter | solution.py:22
  290.4 4.0 copy-start
  294.6 1.0 copy-start.5
  434.7 6.2 copy-start.6
  434.8 6.2 copy-start.3
  445.3 165.6 %all-gather.5.cloned.1.call-start = ((), (), s32[]{:S(2)}) async-start(), calls=%async_computation.7 | async-start | bytes 4718592 | tf_op jit(solution)/shard_map/all_gather | solution.py:25
  534.0 136.4 %all-reduce.9.cloned.1.call-start = ((), (), s32[]{:S(2)}) async-start(), calls=%async_computation.8 | async-start | bytes 4194304 | tf_op jit(solution)/shard_map/psum | solution.py:28
  610.9 6.0 copy-start.8
  670.5 4.0 copy-start.1
  674.7 1.0 copy-start.4
Sparse Core Ops, SparseCore 0:
  16.6 41.6 all-reduce.4
  65.2 88.5 reduce-scatter.2
  156.0 74.7 all-gather.2
  240.8 49.5 all-reduce.6
  445.4 88.5 reduce-scatter.4
  536.1 74.7 all-gather.4
  620.9 49.5 all-reduce.8
where the time goes:
time: 839 us; the launch traced here: 831 us
  waiting for transfers between devices  471 us (56%)
  other arithmetic  247 us (29%)
  matrix products  55.3 us (7%)
  local copies, waits for them, and re-layouts  35 us (4%)
  between operations  19.9 us (2%)
    reduce_scatter x2, waiting for transfers between devices, shards(): lax.psum_scatter(local_factor.astype(jnp.bfloat16), 'tm', scatter_dimensi...  177 us
    another operation x29, other arithmetic, shards(): lower = jnp.linalg.cholesky(gram)  158 us
    all_gather x2, waiting for transfers between devices, shards(): factor = lax.all_gather(part, 'tm', axis=0, tiled=True)  153 us
    psum x2, waiting for transfers between devices, shards(): both = lax.psum(jnp.concatenate([gram, seen], axis=0), 'chan')  98.9 us
    another operation x5, other arithmetic, shards(): lax.linalg.triangular_solve(lower, seen, left_side=False, lower=True, tra...  80.8 us
    psum x1, waiting for transfers between devices, shards(): both = lax.psum(both, 'chan')  41.8 us
    another operation x27, local copies, waits for them, and re-layouts, shards(): lax.linalg.triangular_solve(lower, seen, left_side=False, lower=True, tra...  23.3 us
  transfers between devices with their start and end apart: 7, of which 7 were waited for; matrix products, arithmetic and copies ran while one was open for 0% of the time, Pallas kernels for 0%

commit v1 on v0

--- a/solution.py
+++ b/solution.py
@@ -13,7 +13,9 @@
     norms = jnp.sum(wide * wide, axis=1)
     local = jnp.dot(samples, sketch, preferred_element_type=f32)
     both = jnp.concatenate([local, jnp.broadcast_to(norms[:, None], (rows, 128))], axis=1)
-    both = lax.psum(both, "chan")
+    both = both
+    for hop in (1, 2):
+        both = both + lax.ppermute(both, "chan", [(dev, dev ^ hop) for dev in range(4)])
     sketched, norms = (both[:, :rank], both[:, rank])
     weights = jnp.ones((rows,), f32)
     for step in range(ROUNDS):

time: 839 us -> 840 us (level)
    psum x1 -> x0, waiting for transfers between devices: 41.8 us -> none  [shards(): both = lax.psum(both, 'chan')]
    ppermute x0 -> x2, waiting for transfers between devices: none -> 31.7 us  [shards(): lax.ppermute(both, 'chan', [(dev, dev ^ hop) for dev in range(4)])]
  transfers between devices with their start and end apart: 7 -> 8, of which waited for: 7 -> 8; matrix products, arithmetic and copies ran while one was open for 0% -> 0% of each run, Pallas kernels for 0% -> 0%
where the time goes in v1:
time: 840 us; the launch traced here: 831 us
  waiting for transfers between devices  463 us (55%)
  other arithmetic  248 us (30%)
  matrix products  56.1 us (7%)
  local copies, waits for them, and re-layouts  39.2 us (5%)
  between operations  19.9 us (2%)
    reduce_scatter x2, waiting for transfers between devices, shards(): lax.psum_scatter(local_factor.astype(jnp.bfloat16), 'tm', scatter_dimensi...  179 us
    another operation x29, other arithmetic, shards(): lower = jnp.linalg.cholesky(gram)  158 us
    all_gather x2, waiting for transfers between devices, shards(): factor = lax.all_gather(part, 'tm', axis=0, tiled=True)  153 us
    psum x2, waiting for transfers between devices, shards(): both = lax.psum(jnp.concatenate([gram, seen], axis=0), 'chan')  98.9 us
    another operation x5, other arithmetic, shards(): lax.linalg.triangular_solve(lower, seen, left_side=False, lower=True, tra...  82.3 us
    ppermute x2, waiting for transfers between devices, shards(): lax.ppermute(both, 'chan', [(dev, dev ^ hop) for dev in range(4)])  31.7 us
    another operation x27, local copies, waits for them, and re-layouts, shards(): lax.linalg.triangular_solve(lower, seen, left_side=False, lower=True, tra...  26.4 us
  transfers between devices with their start and end apart: 8, of which 8 were waited for; matrix products, arithmetic and copies ran while one was open for 0% of the time, Pallas kernels for 0%

profile of v1, /device:TPU:0, one launch (start us, length us, event | category | flops | bytes accessed | tf_op | source)
XLA Modules:
  0.0 831.1 jit_solution(5073464191785248919)
XLA Ops:
  21.9 29.1 %collective-permute-done.1 = f32[512,640]{0,1:T(8,128)S(1)} collective-permute-done((f32[512,640]{0,1:T(8,128)S(1)}, f32[512,640]{0,1:T(8,128)S(1)}, u32[]{:S(2)}, u32[]{:S(2)}) %collective-permute-start.1) | collective-permute-done | bytes 1310752 | tf_op jit(solution)/shard_map/ppermute | solution.py:18
  56.6 90.1 %reduce-scatter.3.cloned.1.call-done = bf16[512,512]{0,1:T(8,128)(2,1)} async-done(((bf16[4096,512]{0,1:T(8,128)(2,1)}), bf16[512,512]{0,1:T(8,128)(2,1)}) %reduce-scatter.3.cloned.1.call-update) | async-done | bytes 524304 | tf_op jit(solution)/shard_map/reduce_scatter | solution.py:24
  146.8 77.0 %all-gather.3.cloned.1.call-done = bf16[4096,512]{0,1:T(8,128)(2,1)} async-done(((bf16[512,512]{0,1:T(8,128)(2,1)}), bf16[4096,512]{0,1:T(8,128)(2,1)}) %all-gather.3.cloned.1.call-update) | async-done | bytes 4194320 | tf_op jit(solution)/shard_map/all_gather | solution.py:27
  234.1 49.2 %all-reduce.4.cloned.1.call-done = f32[1024,512]{0,1:T(8,128)} async-done(((f32[1024,512]{0,1:T(8,128)}), f32[1024,512]{0,1:T(8,128)}) %all-reduce.4.cloned.1.call-update) | async-done | bytes 2097168 | tf_op jit(solution)/shard_map/psum | solution.py:30
  288.5 11.7 %cholesky.286 = f32[128,128]{1,0:T(8,128)S(1)} custom-call(f32[128,128]{1,0:T(8,128)S(1)} %cholesky.426), custom_call_target="Cholesky" | custom-call | tf_op jit(solution)/shard_map/jit(cholesky)/cholesky | solution.py:32
  300.2 9.8 %custom-call.27 = f32[1,128,128]{1,2,0:T(8,128)S(1)} custom-call(f32[1,128,128]{2,1,0:T(8,128)S(1)} %get-tuple-element.65), custom_call_target="InvertDiagBlocksLowerTriangular" | custom-call | tf_op jit(solution)/shard_map/jit(cholesky)/cholesky | solution.py:32
  312.7 11.7 %cholesky.305 = f32[128,128]{1,0:T(8,128)S(1)} custom-call(f32[128,128]{1,0:T(8,128)S(1)} %cholesky.430), custom_call_target="Cholesky" | custom-call | tf_op jit(solution)/shard_map/jit(cholesky)/cholesky | solution.py:32
  324.5 10.0 %custom-call.28 = f32[1,128,128]{1,2,0:T(8,128)S(1)} custom-call(f32[1,128,128]{2,1,0:T(8,128)S(1)} %get-tuple-element.62), custom_call_target="InvertDiagBlocksLowerTriangular" | custom-call | tf_op jit(solution)/shard_map/jit(cholesky)/cholesky | solution.py:32
  336.0 11.7 %cholesky.326 = f32[128,128]{1,0:T(8,128)S(1)} custom-call(f32[128,128]{1,0:T(8,128)S(1)} %cholesky.435), custom_call_target="Cholesky" | custom-call | tf_op jit(solution)/shard_map/jit(cholesky)/cholesky | solution.py:32
  348.5 9.8 %custom-call.29 = f32[1,128,128]{1,2,0:T(8,128)S(1)} custom-call(f32[1,128,128]{2,1,0:T(8,128)S(1)} %get-tuple-element.59), custom_call_target="InvertDiagBlocksLowerTriangular" | custom-call | tf_op jit(solution)/shard_map/jit(cholesky)/cholesky | solution.py:32
  359.7 11.7 %cholesky.343 = f32[128,128]{1,0:T(8,128)S(1)} custom-call(f32[128,128]{1,0:T(8,128)S(1)} %convolution_subtract_fusion.11), custom_call_target="Cholesky" | custom-call | tf_op jit(solution)/shard_map/jit(cholesky)/cholesky | solution.py:32
  377.3 14.1 %while.4 = (s32[]{:T(128)}, f32[512,512]{1,0:T(8,128)}, s32[4,2]{0,1:T(2,128)S(1)}, f32[4,128,128]{2,1,0:T(8,128)}, s32[]{:T(128)}) while((s32[]{:T(128)}, f32[512,512]{1,0:T(8,128)}, s32[4,2]{0,1:T(2,128)S(1)}, f32[4,128,128]{2,1,0:T(8,128)}, s32[]{:T(128)}) %tuple.58), condition=%wide.while_cond, body=%wide.while_body.sunk | while | flops 2 | bytes 132705 | solution.py:33
  391.4 40.7 %custom-call.30 = f32[4,128,128]{1,2,0:T(8,128)} custom-call(f32[4,128,128]{2,1,0:T(8,128)} %get-tuple-element.18), custom_call_target="InvertDiagBlocksLowerTriangular" | custom-call | tf_op jit(solution)/shard_map/triangular_solve/custom-call.3 | solution.py:33
  446.0 88.6 %reduce-scatter.5.cloned.1.call-done = bf16[512,512]{0,1:T(8,128)(2,1)} async-done(((bf16[4096,512]{0,1:T(8,128)(2,1)}), bf16[512,512]{0,1:T(8,128)(2,1)}) %reduce-scatter.5.cloned.1.call-update) | async-done | bytes 524304 | tf_op jit(solution)/shard_map/reduce_scatter | solution.py:24
  535.1 76.4 %all-gather.5.cloned.1.call-done = bf16[4096,512]{0,1:T(8,128)(2,1)} async-done(((bf16[512,512]{0,1:T(8,128)(2,1)}), bf16[4096,512]{0,1:T(8,128)(2,1)}) %all-gather.5.cloned.1.call-update) | async-done | bytes 4194320 | tf_op jit(solution)/shard_map/all_gather | solution.py:27
  621.4 49.7 %all-reduce.6.cloned.1.call-done = f32[1024,512]{0,1:T(8,128)} async-done(((f32[1024,512]{0,1:T(8,128)}), f32[1024,512]{0,1:T(8,128)}) %all-reduce.6.cloned.1.call-update) | async-done | bytes 2097168 | tf_op jit(solution)/shard_map/psum | solution.py:30
  676.3 11.7 %cholesky.358 = f32[128,128]{1,0:T(8,128)S(1)} custom-call(f32[128,128]{1,0:T(8,128)S(1)} %cholesky.439), custom_call_target="Cholesky" | custom-call | tf_op jit(solution)/shard_map/jit(cholesky)/cholesky | solution.py:32
  688.2 9.8 %custom-call.31 = f32[1,128,128]{1,2,0:T(8,128)S(1)} custom-call(f32[1,128,128]{2,1,0:T(8,128)S(1)} %get-tuple-element.55), custom_call_target="InvertDiagBlocksLowerTriangular" | custom-call | tf_op jit(solution)/shard_map/jit(cholesky)/cholesky | solution.py:32
  700.5 11.9 %cholesky.377 = f32[128,128]{1,0:T(8,128)S(1)} custom-call(f32[128,128]{1,0:T(8,128)S(1)} %cholesky.443), custom_call_target="Cholesky" | custom-call | tf_op jit(solution)/shard_map/jit(cholesky)/cholesky | solution.py:32
  713.8 9.8 %custom-call.32 = f32[1,128,128]{1,2,0:T(8,128)S(1)} custom-call(f32[1,128,128]{2,1,0:T(8,128)S(1)} %get-tuple-element.52), custom_call_target="InvertDiagBlocksLowerTriangular" | custom-call | tf_op jit(solution)/shard_map/jit(cholesky)/cholesky | solution.py:32
  725.1 11.7 %cholesky.398 = f32[128,128]{1,0:T(8,128)S(1)} custom-call(f32[128,128]{1,0:T(8,128)S(1)} %cholesky.448), custom_call_target="Cholesky" | custom-call | tf_op jit(solution)/shard_map/jit(cholesky)/cholesky | solution.py:32
  749.0 11.7 %cholesky.415 = f32[128,128]{1,0:T(8,128)S(1)} custom-call(f32[128,128]{1,0:T(8,128)S(1)} %convolution_subtract_fusion.10), custom_call_target="Cholesky" | custom-call | tf_op jit(solution)/shard_map/jit(cholesky)/cholesky | solution.py:32
  765.1 11.7 %while.5 = (s32[]{:T(128)}, f32[512,512]{1,0:T(8,128)}, s32[4,2]{0,1:T(2,128)S(1)}, f32[4,128,128]{2,1,0:T(8,128)S(1)}, s32[]{:T(128)}) while((s32[]{:T(128)}, f32[512,512]{1,0:T(8,128)}, s32[4,2]{0,1:T(2,128)S(1)}, f32[4,128,128]{2,1,0:T(8,128)S(1)}, s32[]{:T(128)}) %tuple.76), condition=%wide.while_cond.clone, body=%wide.while_body.clone.sunk | while | flops 2 | bytes 131181 | solution.py:33
  776.8 39.3 %custom-call.34 = f32[4,128,128]{1,2,0:T(8,128)S(1)} custom-call(f32[4,128,128]{2,1,0:T(8,128)S(1)} %get-tuple-element.19), custom_call_target="InvertDiagBlocksLowerTriangular" | custom-call | tf_op jit(solution)/shard_map/triangular_solve/custom-call.3 | solution.py:33
  (140 shorter events, 128.0 us)
Async XLA Ops:
  7.2 139.5 %reduce-scatter.3.cloned.1.call-start = ((), (), s32[]{:S(2)}) async-start(), calls=%async_computation.2 | async-start | bytes 4718592 | tf_op jit(solution)/shard_map/reduce_scatter | solution.py:24
  7.2 3.5 copy-start.2
  15.4 3.2 collective-permute-start
  18.9 32.0 %collective-permute-start.1 = (f32[512,640]{0,1:T(8,128)S(1)}, f32[512,640]{0,1:T(8,128)S(1)}, u32[]{:S(2)}, u32[]{:S(2)}) collective-permute-start(f32[512,640]{0,1:T(8,128)S(1)} %fusion.72), channel_id=1, source_target_pairs={{0,2},{1,3},{2,0},{3,1},{4,6},{5,7},{6,4},{7,5},{8,10},{9,11},{10,... | collective-permute-start | bytes 3932168 | tf_op jit(solution)/shard_map/ppermute | solution.py:18
  51.2 1.1 copy-start.6
  56.6 167.2 %all-gather.3.cloned.1.call-start = ((), (), s32[]{:S(2)}) async-start(), calls=%async_computation.3 | async-start | bytes 4718592 | tf_op jit(solution)/shard_map/all_gather | solution.py:27
  146.7 136.6 %all-reduce.4.cloned.1.call-start = ((), (), s32[]{:S(2)}) async-start(), calls=%async_computation.4 | async-start | bytes 4194304 | tf_op jit(solution)/shard_map/psum | solution.py:30
  223.7 6.0 copy-start.8
  233.6 301.1 %reduce-scatter.5.cloned.1.call-start = ((), (), s32[]{:S(2)}) async-start(), calls=%async_computation.5 | async-start | bytes 4718592 | tf_op jit(solution)/shard_map/reduce_scatter | solution.py:24
  283.3 4.0 copy-start
  287.5 1.0 copy-start.5
  376.6 65.0 %copy-start.7 = (f32[512,640]{0,1:T(8,128)S(1)}, f32[512,640]{0,1:T(8,128)}, u32[]{:S(2)}) copy-start(f32[512,640]{0,1:T(8,128)} %copy-done.6) | copy-start | bytes 3932164
  432.1 9.5 %copy-start.3 = (bf16[512,4096]{1,0:T(8,128)(2,1)S(1)}, bf16[512,4096]{1,0:T(8,128)(2,1)}, u32[]{:S(2)}) copy-start(bf16[512,4096]{1,0:T(8,128)(2,1)} %param.5) | copy-start | bytes 12582916
  446.0 165.6 %all-gather.5.cloned.1.call-start = ((), (), s32[]{:S(2)}) async-start(), calls=%async_computation.6 | async-start | bytes 4718592 | tf_op jit(solution)/shard_map/all_gather | solution.py:27
  534.7 136.4 %all-reduce.6.cloned.1.call-start = ((), (), s32[]{:S(2)}) async-start(), calls=%async_computation.7 | async-start | bytes 4194304 | tf_op jit(solution)/shard_map/psum | solution.py:30
  611.5 6.0 copy-start.9
  671.1 4.0 copy-start.1
  675.3 1.0 copy-start.4
Sparse Core Ops, SparseCore 0:
  56.7 89.9 reduce-scatter.2
  148.9 74.7 all-gather.2
  233.7 49.5 all-reduce.3
  446.1 88.5 reduce-scatter.4
  536.7 74.7 all-gather.4
  621.5 49.5 all-reduce.5
